TPU v7x, 32 devices: a whole 2x2x4 slice. The times are simulated.
32 devices in a mesh: seg: 4 (over z), sec: 8 (over y, x, core).
Axes of the slice: x: 2, y: 2, z: 4, core: 2. Of those that a mesh axis runs over, the one named last changes fastest.
Arguments:
- start_vector: float32 [4, 1024, 2, 1024], P('seg', 'sec'), may hold values from -6 to 6
- left_env: bfloat16 [4, 5, 1024, 1024], P('seg', None, 'sec'), as said below
- right_env: bfloat16 [4, 5, 1024, 1024], P('seg', None, 'sec'), as said below
- charge_left: int32 [4, 1024], P('seg', 'sec'), may hold values from -8 to 8, as said below
- charge_right: int32 [4, 1024], P('seg'), may hold values from -8 to 8, as said below
Outputs:
- final_vector: float32 [4, 1024, 2, 1024], P('seg', 'sec')
- coefficients: float32 [4, 4], P('seg')
Inputs may be any that keep to these rules, and one draw needn't show every extreme that they name: `charge_left`: each segment's left bond holds both charges -8 and 8; charges gather near 0. `charge_right`: each segment's right bond holds both charges -8 and 8; charges gather near 0. left_env[g] is zero outside the charge rule stated for it, with the charges charge_left[(g + 1) mod 4]. right_env[g] is zero outside the charge rule stated for it, with the charges charge_right[(g - 1) mod 4].
All inputs are finite; a program needn't handle non-finite values.
Results may differ from a plain program's by a relative error of at most 0.0042.
Values may be sent and summed in bfloat16 or wider, within the bound.
A program may use at most 128 MiB of HBM per device.

v0:
```python
import jax
import jax.numpy as jnp
from jax import lax
from jax.sharding import PartitionSpec as P

CHI = 1024
ITERS = 4
EPS = 1e-06


def shifted(value, axis, steps):
    count = lax.axis_size(axis)
    pairs = [(source, (source + steps) % count) for source in range(count)]
    return lax.ppermute(value, axis, pairs)


def merged(env):
    return jnp.stack([env[0] + env[1] + env[2], env[3], env[4]])


def on_device(start_vector, left_env, right_env, charge_left, charge_right):
    left = shifted(merged(left_env[0]), "seg", 1)
    passed = shifted(merged(right_env[0]), "seg", -1)
    right = lax.all_gather(passed, "sec", axis=1, tiled=True)
    charges = charge_right[0]
    step = charges[None, :] - charges[:, None]
    right_stack = jnp.concatenate(
        [
            jnp.where(step == 0, right[0], 0),
            jnp.where(step == 1, right[0], 0),
            jnp.where(step == -1, right[0], 0),
            right[1],
            right[2],
        ],
        axis=0,
    )
    gap = charges[None, :] - charge_left[0][:, None]
    down, up = (gap == 0, gap == 1)
    allowed = down | up
    spin = jnp.where(up, 0.5, -0.5)
    rows = gap.shape[0]
    left_rows = left.reshape(3 * rows, left.shape[2])
    current = jnp.where(down, start_vector[0, :, 0], jnp.where(up, start_vector[0, :, 1], 0.0))
    norm = lax.psum(jnp.sum(current * current), "sec")
    current = current / jnp.sqrt(norm + EPS)
    previous = jnp.zeros_like(current)
    beta = jnp.float32(0.0)
    betas = []
    for _ in range(ITERS):
        whole = lax.all_gather(current.astype(jnp.bfloat16), "sec", axis=0, tiled=True)
        first = jnp.dot(left_rows, whole, preferred_element_type=jnp.float32)
        first = first.reshape(3, rows, -1)
        half = 0.5 * first[2]
        mixed = jnp.concatenate(
            [
                jnp.where(allowed, first[0] + spin * first[1], 0.0),
                jnp.where(up, half, 0.0),
                jnp.where(down, half, 0.0),
                jnp.where(allowed, spin * first[2], 0.0),
                jnp.where(allowed, first[2], 0.0),
            ],
            axis=1,
        ).astype(jnp.bfloat16)
        image = jnp.dot(mixed, right_stack, preferred_element_type=jnp.float32)
        residual = jnp.where(allowed, image, 0.0) - beta * previous
        alpha = lax.psum(jnp.sum(residual * current), "sec")
        residual = residual - alpha * current
        beta = jnp.sqrt(lax.psum(jnp.sum(residual * residual), "sec") + EPS)
        previous = current
        current = residual / beta
        betas.append(beta)
    scaled = current * CHI
    final = jnp.stack([jnp.where(down, scaled, 0.0), jnp.where(up, scaled, 0.0)], axis=1)
    return (final[None], jnp.stack(betas)[None])


def solution(mesh):
    return jax.shard_map(
        on_device,
        mesh=mesh,
        in_specs=(
            P("seg", "sec", None, None),
            P("seg", None, "sec", None),
            P("seg", None, "sec", None),
            P("seg", "sec"),
            P("seg", None),
        ),
        out_specs=(P("seg", "sec", None, None), P("seg", None)),
        check_vma=False,
    )
```

profile of v0, /device:TPU:0, one launch (start us, length us, event | category | flops | bytes accessed | tf_op | source)
XLA Modules:
  0.0 353.4 jit_solution(2616346199038595305)
XLA Ops:
  7.2 2.5 fusion.78
  9.8 1.0 multiply_reduce_fusion.8
  10.7 15.8 %psum.63 = f32[]{:T(128)} all-reduce(f32[]{:T(128)} %multiply_reduce_fusion.8), channel_id=1, replica_groups=mesh['seg'=4,'sec'=8] {'sec'}, use_global_device_ids=true, to_apply=%region_1.2 | all-reduce | flops 1 | bytes 8 | tf_op jit(solution)/shard_map/psum | solution.py:44
  27.2 1.0 fusion.77
  28.5 3.7 %collective-permute-start.1 = (bf16[3,128,1024]{2,1,0:T(8,128)(2,1)S(1)}, bf16[3,128,1024]{2,1,0:T(8,128)(2,1)S(1)}, u32[]{:S(2)}, u32[]{:S(2)}) collective-permute-start(bf16[3,128,1024]{2,1,0:T(8,128)(2,1)S(1)} %pad_maximum_fusion.1), channel_id=1, source_target_pairs={{0,24},{8,0},{16,8},{24,16},{1,25},{9,1},{17,9},{25,17},{2,26},{10... | collective-permute-start | bytes 2359304 | tf_op jit(solution)/shard_map/ppermute | solution.py:14
  32.1 16.1 %collective-permute-done.1 = bf16[3,128,1024]{2,1,0:T(8,128)(2,1)S(1)} collective-permute-done((bf16[3,128,1024]{2,1,0:T(8,128)(2,1)S(1)}, bf16[3,128,1024]{2,1,0:T(8,128)(2,1)S(1)}, u32[]{:S(2)}, u32[]{:S(2)}) %collective-permute-start.1) | collective-permute-done | bytes 786464 | tf_op jit(solution)/shard_map/ppermute | solution.py:14
  48.2 0.9 copy-done.5
  49.4 18.0 %collective-permute-done = bf16[3,128,1024]{2,1,0:T(8,128)(2,1)S(1)} collective-permute-done((bf16[3,128,1024]{2,1,0:T(8,128)(2,1)S(1)}, bf16[3,128,1024]{2,1,0:T(8,128)(2,1)S(1)}, u32[]{:S(2)}, u32[]{:S(2)}) %collective-permute-start) | collective-permute-done | bytes 786464 | tf_op jit(solution)/shard_map/ppermute | solution.py:14
  67.4 2.6 fusion.79
  70.0 0.2 fusion.65
  70.5 0.2 fusion.64
  70.8 32.6 %all-gather.8.cloned.1.call-done = bf16[3,1024,1024]{2,1,0:T(8,128)(2,1)} async-done(((bf16[3,128,1024]{2,1,0:T(8,128)(2,1)}), bf16[3,1024,1024]{2,1,0:T(8,128)(2,1)}) %all-gather.8.cloned.1.call-update) | async-done | bytes 6291472 | tf_op jit(solution)/shard_map/all_gather | solution.py:24
  103.4 2.4 fusion.5
  105.8 2.3 fusion.4
  108.1 0.7 fusion.3
  109.2 2.8 multiply_reduce_fusion.7
  112.0 1.2 copy-done
  113.2 13.7 %psum.64 = f32[]{:T(128)} all-reduce(f32[]{:T(128)} %get-tuple-element.22), channel_id=1, replica_groups=mesh['seg'=4,'sec'=8] {'sec'}, use_global_device_ids=true, to_apply=%region_3.4 | all-reduce | flops 1 | bytes 8 | tf_op jit(solution)/shard_map/psum | solution.py:66
  126.9 1.4 multiply_reduce_fusion.6
  128.3 12.4 %psum.65 = f32[]{:T(128)} all-reduce(f32[]{:T(128)} %multiply_reduce_fusion.6), channel_id=1, replica_groups=mesh['seg'=4,'sec'=8] {'sec'}, use_global_device_ids=true, to_apply=%region_5.6 | all-reduce | flops 1 | bytes 8 | tf_op jit(solution)/shard_map/psum | solution.py:68
  141.4 1.5 fusion.76
  142.9 27.9 %all-gather.10.cloned.1.call-done = bf16[1024,1024]{1,0:T(8,128)(2,1)} async-done(((bf16[128,1024]{1,0:T(8,128)(2,1)}), bf16[1024,1024]{1,0:T(8,128)(2,1)}) %all-gather.10.cloned.1.call-update) | async-done | bytes 2097168 | tf_op jit(solution)/shard_map/all_gather | solution.py:50
  170.8 2.6 fusion.80
  173.4 0.2 fusion.63
  174.2 6.3 %multiply_reduce_fusion.5 = (f32[]{:T(128)}, f32[128,1024]{1,0:T(8,128)S(1)}) fusion(f32[128,1024]{1,0:T(8,128)S(1)} %get-tuple-element.9, f32[128,1024]{1,0:T(8,128)S(1)} %get-tuple-element.11, f32[]{:T(128)} %sqrt.16, bf16[128,5120]{1,0:T(8,128)(2,1)S(1)} %fusion.55, bf16[5120,1024]{1,0:T(8,128)(2,1)} %copy-done, s32[128]{0:T(128)S(1)} %bitcast.120, ...), kind=kOutput, calls=%fused_computation.90 | convolution fusion | flops 1343356928 | bytes 13373960 | tf_op jit(solution)/shard_map/dot_general | solution.py:64
  180.6 13.7 %psum.66 = f32[]{:T(128)} all-reduce(f32[]{:T(128)} %get-tuple-element.24), channel_id=1, replica_groups=mesh['seg'=4,'sec'=8] {'sec'}, use_global_device_ids=true, to_apply=%region_7.8 | all-reduce | flops 1 | bytes 8 | tf_op jit(solution)/shard_map/psum | solution.py:66
  194.3 1.4 multiply_reduce_fusion.4
  195.7 12.4 %psum.67 = f32[]{:T(128)} all-reduce(f32[]{:T(128)} %multiply_reduce_fusion.4), channel_id=1, replica_groups=mesh['seg'=4,'sec'=8] {'sec'}, use_global_device_ids=true, to_apply=%region_9.10 | all-reduce | flops 1 | bytes 8 | tf_op jit(solution)/shard_map/psum | solution.py:68
  208.8 1.5 fusion.75
  210.3 0.2 all-gather.14.cloned.1.call-start
  210.5 27.7 %all-gather.12.cloned.1.call-done = bf16[1024,1024]{1,0:T(8,128)(2,1)} async-done(((bf16[128,1024]{1,0:T(8,128)(2,1)}), bf16[1024,1024]{1,0:T(8,128)(2,1)}) %all-gather.12.cloned.1.call-update) | async-done | bytes 2097168 | tf_op jit(solution)/shard_map/all_gather | solution.py:50
  238.2 2.6 fusion.81
  240.8 0.2 fusion.61
  241.6 6.3 %multiply_reduce_fusion.3 = (f32[]{:T(128)}, f32[128,1024]{1,0:T(8,128)S(1)}) fusion(f32[128,1024]{1,0:T(8,128)S(1)} %get-tuple-element.7, f32[128,1024]{1,0:T(8,128)S(1)} %get-tuple-element.9, f32[]{:T(128)} %sqrt.17, bf16[128,5120]{1,0:T(8,128)(2,1)S(1)} %fusion.56, bf16[5120,1024]{1,0:T(8,128)(2,1)} %copy-done, s32[128]{0:T(128)S(1)} %bitcast.126, ...), kind=kOutput, calls=%fused_computation.86 | convolution fusion | flops 1343356928 | bytes 13373960 | tf_op jit(solution)/shard_map/dot_general | solution.py:64
  248.0 13.7 %psum.68 = f32[]{:T(128)} all-reduce(f32[]{:T(128)} %get-tuple-element.26), channel_id=1, replica_groups=mesh['seg'=4,'sec'=8] {'sec'}, use_global_device_ids=true, to_apply=%region_11.12 | all-reduce | flops 1 | bytes 8 | tf_op jit(solution)/shard_map/psum | solution.py:66
  261.7 1.4 multiply_reduce_fusion.2
  263.1 12.4 %psum.69 = f32[]{:T(128)} all-reduce(f32[]{:T(128)} %multiply_reduce_fusion.2), channel_id=1, replica_groups=mesh['seg'=4,'sec'=8] {'sec'}, use_global_device_ids=true, to_apply=%region_13.14 | all-reduce | flops 1 | bytes 8 | tf_op jit(solution)/shard_map/psum | solution.py:68
  276.2 1.5 fusion.74
  277.6 27.9 %all-gather.14.cloned.1.call-done = bf16[1024,1024]{1,0:T(8,128)(2,1)} async-done(((bf16[128,1024]{1,0:T(8,128)(2,1)}), bf16[1024,1024]{1,0:T(8,128)(2,1)}) %all-gather.14.cloned.1.call-update) | async-done | bytes 2097168 | tf_op jit(solution)/shard_map/all_gather | solution.py:50
  305.6 2.6 fusion.82
  308.2 0.2 fusion.59
  309.0 6.3 %multiply_reduce_fusion.1 = (f32[]{:T(128)}, f32[128,1024]{1,0:T(8,128)S(1)}) fusion(f32[128,1024]{1,0:T(8,128)S(1)} %get-tuple-element.5, f32[128,1024]{1,0:T(8,128)S(1)} %get-tuple-element.7, f32[]{:T(128)} %sqrt.18, bf16[128,5120]{1,0:T(8,128)(2,1)S(1)} %fusion.57, bf16[5120,1024]{1,0:T(8,128)(2,1)} %copy-done, s32[128]{0:T(128)S(1)} %bitcast.132, ...), kind=kOutput, calls=%fused_computation.82 | convolution fusion | flops 1343356928 | bytes 13373960 | tf_op jit(solution)/shard_map/dot_general | solution.py:64
  315.4 13.7 %psum.70 = f32[]{:T(128)} all-reduce(f32[]{:T(128)} %get-tuple-element.28), channel_id=1, replica_groups=mesh['seg'=4,'sec'=8] {'sec'}, use_global_device_ids=true, to_apply=%region_15.16 | all-reduce | flops 1 | bytes 8 | tf_op jit(solution)/shard_map/psum | solution.py:66
  329.1 1.4 multiply_reduce_fusion
  330.4 12.4 %psum.71 = f32[]{:T(128)} all-reduce(f32[]{:T(128)} %multiply_reduce_fusion), channel_id=1, replica_groups=mesh['seg'=4,'sec'=8] {'sec'}, use_global_device_ids=true, to_apply=%region_17.18 | all-reduce | flops 1 | bytes 8 | tf_op jit(solution)/shard_map/psum | solution.py:68
  343.5 0.8 fusion.28
  344.5 1.8 copy.9
  346.3 0.6 maximum_bitcast_fusion.1
  (45 shorter events, 3.3 us)
Async XLA Ops:
  7.2 2.6 copy-start.2
  7.2 2.6 copy-start.6
  7.2 60.2 %all-gather.6.cloned.1.call-start = ((), (), s32[]{:S(2)}) async-start(), calls=%async_computation | async-start | bytes 2359296 | tf_op jit(solution)/shard_map/all_gather | solution.py:50
  9.8 18.5 %copy-start.3 = (bf16[1,5,128,1024]{3,2,1,0:T(8,128)(2,1)S(1)}, bf16[1,5,128,1024]{3,2,1,0:T(8,128)(2,1)}, u32[]{:S(2)}) copy-start(bf16[1,5,128,1024]{3,2,1,0:T(8,128)(2,1)} %param.7) | copy-start | bytes 3932164
  28.2 75.2 %all-gather.8.cloned.1.call-start = ((), (), s32[]{:S(2)}) async-start(), calls=%async_computation.1 | async-start | bytes 7077888 | tf_op jit(solution)/shard_map/all_gather | solution.py:24
  28.4 20.8 %copy-start.4 = (bf16[1,5,128,1024]{3,2,1,0:T(8,128)(2,1)S(1)}, bf16[1,5,128,1024]{3,2,1,0:T(8,128)(2,1)}, u32[]{:S(2)}) copy-start(bf16[1,5,128,1024]{3,2,1,0:T(8,128)(2,1)} %param.6) | copy-start | bytes 3932164
  28.5 19.7 %collective-permute-start.1 = (bf16[3,128,1024]{2,1,0:T(8,128)(2,1)S(1)}, bf16[3,128,1024]{2,1,0:T(8,128)(2,1)S(1)}, u32[]{:S(2)}, u32[]{:S(2)}) collective-permute-start(bf16[3,128,1024]{2,1,0:T(8,128)(2,1)S(1)} %pad_maximum_fusion.1), channel_id=1, source_target_pairs={{0,24},{8,0},{16,8},{24,16},{1,25},{9,1},{17,9},{25,17},{2,26},{10... | collective-permute-start | bytes 2359304 | tf_op jit(solution)/shard_map/ppermute | solution.py:14
  48.2 0.9 copy-start.5
  49.1 121.7 %all-gather.10.cloned.1.call-start = ((), (), s32[]{:S(2)}) async-start(), calls=%async_computation.2 | async-start | bytes 2359296 | tf_op jit(solution)/shard_map/all_gather | solution.py:50
  49.3 18.1 %collective-permute-start = (bf16[3,128,1024]{2,1,0:T(8,128)(2,1)S(1)}, bf16[3,128,1024]{2,1,0:T(8,128)(2,1)S(1)}, u32[]{:S(2)}, u32[]{:S(2)}) collective-permute-start(bf16[3,128,1024]{2,1,0:T(8,128)(2,1)S(1)} %pad_maximum_fusion), channel_id=1, source_target_pairs={{0,8},{8,16},{16,24},{24,0},{1,9},{9,17},{17,25},{25,1},{2,10},{10... | collective-permute-start | bytes 2359304 | tf_op jit(solution)/shard_map/ppermute | solution.py:14
  103.4 4.7 %copy-start.1 = (bf16[3,1024,1024]{2,1,0:T(8,128)(2,1)S(1)}, bf16[3,1024,1024]{2,1,0:T(8,128)(2,1)}, u32[]{:S(2)}) copy-start(bf16[3,1024,1024]{2,1,0:T(8,128)(2,1)} %all-gather.8.cloned.1.call-done) | copy-start | bytes 18874372
  109.2 4.0 %copy-start = (bf16[5120,1024]{1,0:T(8,128)(2,1)}, bf16[5120,1024]{1,0:T(8,128)(2,1)S(1)}, u32[]{:S(2)}) copy-start(bf16[5120,1024]{1,0:T(8,128)(2,1)S(1)} %fusion.6) | copy-start | bytes 31457284
  142.9 95.3 %all-gather.12.cloned.1.call-start = ((), (), s32[]{:S(2)}) async-start(), calls=%async_computation.3 | async-start | bytes 2359296 | tf_op jit(solution)/shard_map/all_gather | solution.py:50
  210.3 95.3 %all-gather.14.cloned.1.call-start = ((), (), s32[]{:S(2)}) async-start(), calls=%async_computation.4 | async-start | bytes 2359296 | tf_op jit(solution)/shard_map/all_gather | solution.py:50
Sparse Core Ops, SparseCore 0:
  28.3 27.1 all-gather.5
  58.0 45.3 all-gather.7
  143.0 27.7 all-gather.9
  210.4 27.7 all-gather.11
  277.8 27.7 all-gather.13
where the time goes:
time: 354 us; the launch traced here: 353 us
  waiting for transfers between devices  150 us (42%)
  blocking collectives  120 us (34%)
  matrix products  32.1 us (9%)
  other arithmetic  22.3 us (6%)
  between operations  17.6 us (5%)
  local copies, waits for them, and re-layouts  6.75 us (2%)
  starting transfers between devices  4.1 us (1%)
    all_gather x4, waiting for transfers between devices, on_device(): lax.all_gather(current.astype(jnp.bfloat16), 'sec', axis=0, tiled=True)  83.5 us
    psum x4, blocking collectives, on_device(): alpha = lax.psum(jnp.sum(residual * current), 'sec')  54.8 us
    psum x4, blocking collectives, on_device(): beta = jnp.sqrt(lax.psum(jnp.sum(residual * residual), 'sec') + EPS)  49.6 us
    ppermute x2, waiting for transfers between devices, shifted(): return lax.ppermute(value, axis, pairs)  34.1 us
    all_gather x1, waiting for transfers between devices, on_device(): right = lax.all_gather(passed, 'sec', axis=1, tiled=True)  32.6 us
    dot_general x4, matrix products, on_device(): image = jnp.dot(mixed, right_stack, preferred_element_type=jnp.float32)  21.8 us
    psum x1, blocking collectives, on_device(): norm = lax.psum(jnp.sum(current * current), 'sec')  15.8 us
    dot_general x4, matrix products, on_device(): first = jnp.dot(left_rows, whole, preferred_element_type=jnp.float32)  10.3 us
  transfers between devices with their start and end apart: 7, of which 6 were waited for; matrix products, arithmetic and copies ran while one was open for 1% of the time, Pallas kernels for 0%

commit v1 on v0

--- a/solution.py
+++ b/solution.py
@@ -21,7 +21,7 @@
 def on_device(start_vector, left_env, right_env, charge_left, charge_right):
     left = shifted(merged(left_env[0]), "seg", 1)
     passed = shifted(merged(right_env[0]), "seg", -1)
-    right = lax.all_gather(passed, "sec", axis=1, tiled=True)
+    right = jnp.concatenate(lax.all_gather(passed, "sec"), axis=1)
     charges = charge_right[0]
     step = charges[None, :] - charges[:, None]
     right_stack = jnp.concatenate(

time: 354 us -> 355 us (level)
  local copies, waits for them, and re-layouts: 6.75 us -> 10.7 us
    slice x0 -> x1, local copies, waits for them, and re-layouts: none -> 3.93 us  [on_device(): right[2]]
where the time goes in v1:
time: 355 us; the launch traced here: 354 us
  waiting for transfers between devices  150 us (42%)
  blocking collectives  120 us (34%)
  matrix products  32.1 us (9%)
  other arithmetic  19 us (5%)
  between operations  17.6 us (5%)
  local copies, waits for them, and re-layouts  10.7 us (3%)
  starting transfers between devices  4.1 us (1%)
    all_gather x4, waiting for transfers between devices, on_device(): lax.all_gather(current.astype(jnp.bfloat16), 'sec', axis=0, tiled=True)  83.5 us
    psum x4, blocking collectives, on_device(): alpha = lax.psum(jnp.sum(residual * current), 'sec')  54.8 us
    psum x4, blocking collectives, on_device(): beta = jnp.sqrt(lax.psum(jnp.sum(residual * residual), 'sec') + EPS)  49.6 us
    ppermute x2, waiting for transfers between devices, shifted(): return lax.ppermute(value, axis, pairs)  34.1 us
    all_gather x1, waiting for transfers between devices, on_device(): right = jnp.concatenate(lax.all_gather(passed, 'sec'), axis=1)  32.6 us
    dot_general x4, matrix products, on_device(): image = jnp.dot(mixed, right_stack, preferred_element_type=jnp.float32)  21.8 us
    psum x1, blocking collectives, on_device(): norm = lax.psum(jnp.sum(current * current), 'sec')  15.8 us
    dot_general x4, matrix products, on_device(): first = jnp.dot(left_rows, whole, preferred_element_type=jnp.float32)  10.3 us
  transfers between devices with their start and end apart: 7, of which 6 were waited for; matrix products, arithmetic and copies ran while one was open for 1% of the time, Pallas kernels for 0%

profile of v1, /device:TPU:0, one launch (start us, length us, event | category | flops | bytes accessed | tf_op | source)
XLA Modules:
  0.0 353.9 jit_solution(15007221326425469855)
XLA Ops:
  7.2 2.5 fusion.77
  9.8 1.0 multiply_reduce_fusion.8
  10.7 15.8 %psum.63 = f32[]{:T(128)} all-reduce(f32[]{:T(128)} %multiply_reduce_fusion.8), channel_id=1, replica_groups=mesh['seg'=4,'sec'=8] {'sec'}, use_global_device_ids=true, to_apply=%region_1.2 | all-reduce | flops 1 | bytes 8 | tf_op jit(solution)/shard_map/psum | solution.py:44
  27.2 1.0 fusion.75
  28.5 3.7 %collective-permute-start.1 = (bf16[3,128,1024]{2,1,0:T(8,128)(2,1)S(1)}, bf16[3,128,1024]{2,1,0:T(8,128)(2,1)S(1)}, u32[]{:S(2)}, u32[]{:S(2)}) collective-permute-start(bf16[3,128,1024]{2,1,0:T(8,128)(2,1)S(1)} %pad_maximum_fusion.1), channel_id=1, source_target_pairs={{0,24},{8,0},{16,8},{24,16},{1,25},{9,1},{17,9},{25,17},{2,26},{10... | collective-permute-start | bytes 2359304 | tf_op jit(solution)/shard_map/ppermute | solution.py:14
  32.1 16.1 %collective-permute-done.1 = bf16[3,128,1024]{2,1,0:T(8,128)(2,1)S(1)} collective-permute-done((bf16[3,128,1024]{2,1,0:T(8,128)(2,1)S(1)}, bf16[3,128,1024]{2,1,0:T(8,128)(2,1)S(1)}, u32[]{:S(2)}, u32[]{:S(2)}) %collective-permute-start.1) | collective-permute-done | bytes 786464 | tf_op jit(solution)/shard_map/ppermute | solution.py:14
  48.2 0.9 copy-done.4
  49.4 18.0 %collective-permute-done = bf16[3,128,1024]{2,1,0:T(8,128)(2,1)S(1)} collective-permute-done((bf16[3,128,1024]{2,1,0:T(8,128)(2,1)S(1)}, bf16[3,128,1024]{2,1,0:T(8,128)(2,1)S(1)}, u32[]{:S(2)}, u32[]{:S(2)}) %collective-permute-start) | collective-permute-done | bytes 786464 | tf_op jit(solution)/shard_map/ppermute | solution.py:14
  67.4 2.6 fusion.78
  70.0 0.2 fusion.63
  70.8 32.6 %all-gather.15.cloned.1.call-done = bf16[24,128,1024]{2,1,0:T(8,128)(2,1)} async-done(((bf16[3,128,1024]{2,1,0:T(8,128)(2,1)}), bf16[24,128,1024]{2,1,0:T(8,128)(2,1)}) %all-gather.15.cloned.1.call-update) | async-done | bytes 6291472 | tf_op jit(solution)/shard_map/all_gather | solution.py:24
  103.4 3.9 %fusion.76 = (bf16[1,8,128,1024]{3,2,0,1:T(8,128)(2,1)S(1)}, bf16[1,8,128,1024]{3,2,0,1:T(8,128)(2,1)S(1)}, bf16[1,8,128,1024]{3,2,0,1:T(8,128)(2,1)S(1)}) fusion(bf16[3,8,128,1024]{3,2,0,1:T(8,128)(2,1)} %bitcast.72), kind=kLoop, calls=%fused_computation.129 | loop fusion | bytes 12582912 | tf_op jit(solution)/shard_map/slice | solution.py:33
  107.3 0.7 fusion.5
  108.0 0.7 fusion.4
  108.7 0.7 fusion.3
  109.8 2.8 multiply_reduce_fusion.7
  112.5 1.2 copy-done
  113.7 13.7 %psum.64 = f32[]{:T(128)} all-reduce(f32[]{:T(128)} %get-tuple-element.27), channel_id=1, replica_groups=mesh['seg'=4,'sec'=8] {'sec'}, use_global_device_ids=true, to_apply=%region_3.4 | all-reduce | flops 1 | bytes 8 | tf_op jit(solution)/shard_map/psum | solution.py:66
  127.5 1.4 multiply_reduce_fusion.6
  128.8 12.4 %psum.65 = f32[]{:T(128)} all-reduce(f32[]{:T(128)} %multiply_reduce_fusion.6), channel_id=1, replica_groups=mesh['seg'=4,'sec'=8] {'sec'}, use_global_device_ids=true, to_apply=%region_5.6 | all-reduce | flops 1 | bytes 8 | tf_op jit(solution)/shard_map/psum | solution.py:68
  142.0 1.5 fusion.74
  143.4 0.2 all-gather.11.cloned.1.call-start
  143.7 27.7 %all-gather.9.cloned.1.call-done = bf16[1024,1024]{1,0:T(8,128)(2,1)} async-done(((bf16[128,1024]{1,0:T(8,128)(2,1)}), bf16[1024,1024]{1,0:T(8,128)(2,1)}) %all-gather.9.cloned.1.call-update) | async-done | bytes 2097168 | tf_op jit(solution)/shard_map/all_gather | solution.py:50
  171.4 2.6 fusion.79
  174.0 0.2 fusion.61
  174.8 6.3 %multiply_reduce_fusion.5 = (f32[]{:T(128)}, f32[128,1024]{1,0:T(8,128)S(1)}) fusion(f32[128,1024]{1,0:T(8,128)S(1)} %get-tuple-element.11, f32[128,1024]{1,0:T(8,128)S(1)} %get-tuple-element.13, f32[]{:T(128)} %sqrt.16, bf16[128,5120]{1,0:T(8,128)(2,1)S(1)} %fusion.53, bf16[5120,1024]{1,0:T(8,128)(2,1)} %copy-done, s32[128]{0:T(128)S(1)} %bitcast.116, ...), kind=kOutput, calls=%fused_computation.85 | convolution fusion | flops 1343356928 | bytes 13373960 | tf_op jit(solution)/shard_map/dot_general | solution.py:64
  181.1 13.7 %psum.66 = f32[]{:T(128)} all-reduce(f32[]{:T(128)} %get-tuple-element.29), channel_id=1, replica_groups=mesh['seg'=4,'sec'=8] {'sec'}, use_global_device_ids=true, to_apply=%region_7.8 | all-reduce | flops 1 | bytes 8 | tf_op jit(solution)/shard_map/psum | solution.py:66
  194.8 1.4 multiply_reduce_fusion.4
  196.2 12.4 %psum.67 = f32[]{:T(128)} all-reduce(f32[]{:T(128)} %multiply_reduce_fusion.4), channel_id=1, replica_groups=mesh['seg'=4,'sec'=8] {'sec'}, use_global_device_ids=true, to_apply=%region_9.10 | all-reduce | flops 1 | bytes 8 | tf_op jit(solution)/shard_map/psum | solution.py:68
  209.3 1.5 fusion.73
  210.9 27.9 %all-gather.11.cloned.1.call-done = bf16[1024,1024]{1,0:T(8,128)(2,1)} async-done(((bf16[128,1024]{1,0:T(8,128)(2,1)}), bf16[1024,1024]{1,0:T(8,128)(2,1)}) %all-gather.11.cloned.1.call-update) | async-done | bytes 2097168 | tf_op jit(solution)/shard_map/all_gather | solution.py:50
  238.8 2.6 fusion.80
  241.3 0.2 fusion.59
  242.2 6.3 %multiply_reduce_fusion.3 = (f32[]{:T(128)}, f32[128,1024]{1,0:T(8,128)S(1)}) fusion(f32[128,1024]{1,0:T(8,128)S(1)} %get-tuple-element.9, f32[128,1024]{1,0:T(8,128)S(1)} %get-tuple-element.11, f32[]{:T(128)} %sqrt.17, bf16[128,5120]{1,0:T(8,128)(2,1)S(1)} %fusion.54, bf16[5120,1024]{1,0:T(8,128)(2,1)} %copy-done, s32[128]{0:T(128)S(1)} %bitcast.122, ...), kind=kOutput, calls=%fused_computation.81 | convolution fusion | flops 1343356928 | bytes 13373960 | tf_op jit(solution)/shard_map/dot_general | solution.py:64
  248.5 13.7 %psum.68 = f32[]{:T(128)} all-reduce(f32[]{:T(128)} %get-tuple-element.31), channel_id=1, replica_groups=mesh['seg'=4,'sec'=8] {'sec'}, use_global_device_ids=true, to_apply=%region_11.12 | all-reduce | flops 1 | bytes 8 | tf_op jit(solution)/shard_map/psum | solution.py:66
  262.2 1.4 multiply_reduce_fusion.2
  263.6 12.4 %psum.69 = f32[]{:T(128)} all-reduce(f32[]{:T(128)} %multiply_reduce_fusion.2), channel_id=1, replica_groups=mesh['seg'=4,'sec'=8] {'sec'}, use_global_device_ids=true, to_apply=%region_13.14 | all-reduce | flops 1 | bytes 8 | tf_op jit(solution)/shard_map/psum | solution.py:68
  276.7 1.5 fusion.72
  278.2 27.9 %all-gather.13.cloned.1.call-done = bf16[1024,1024]{1,0:T(8,128)(2,1)} async-done(((bf16[128,1024]{1,0:T(8,128)(2,1)}), bf16[1024,1024]{1,0:T(8,128)(2,1)}) %all-gather.13.cloned.1.call-update) | async-done | bytes 2097168 | tf_op jit(solution)/shard_map/all_gather | solution.py:50
  306.1 2.6 fusion.81
  308.7 0.2 fusion.57
  309.6 6.3 %multiply_reduce_fusion.1 = (f32[]{:T(128)}, f32[128,1024]{1,0:T(8,128)S(1)}) fusion(f32[128,1024]{1,0:T(8,128)S(1)} %get-tuple-element.7, f32[128,1024]{1,0:T(8,128)S(1)} %get-tuple-element.9, f32[]{:T(128)} %sqrt.18, bf16[128,5120]{1,0:T(8,128)(2,1)S(1)} %fusion.55, bf16[5120,1024]{1,0:T(8,128)(2,1)} %copy-done, s32[128]{0:T(128)S(1)} %bitcast.128, ...), kind=kOutput, calls=%fused_computation.77 | convolution fusion | flops 1343356928 | bytes 13373960 | tf_op jit(solution)/shard_map/dot_general | solution.py:64
  315.9 13.7 %psum.70 = f32[]{:T(128)} all-reduce(f32[]{:T(128)} %get-tuple-element.33), channel_id=1, replica_groups=mesh['seg'=4,'sec'=8] {'sec'}, use_global_device_ids=true, to_apply=%region_15.16 | all-reduce | flops 1 | bytes 8 | tf_op jit(solution)/shard_map/psum | solution.py:66
  329.6 1.4 multiply_reduce_fusion
  331.0 12.4 %psum.71 = f32[]{:T(128)} all-reduce(f32[]{:T(128)} %multiply_reduce_fusion), channel_id=1, replica_groups=mesh['seg'=4,'sec'=8] {'sec'}, use_global_device_ids=true, to_apply=%region_17.18 | all-reduce | flops 1 | bytes 8 | tf_op jit(solution)/shard_map/psum | solution.py:68
  344.1 0.8 fusion.26
  345.0 1.8 copy.12
  346.8 0.6 maximum_bitcast_fusion.1
  (44 shorter events, 3.5 us)
Async XLA Ops:
  7.2 2.6 copy-start.1
  7.2 2.6 copy-start.5
  7.2 60.2 %all-gather.7.cloned.1.call-start = ((), (), s32[]{:S(2)}) async-start(), calls=%async_computation | async-start | bytes 2359296 | tf_op jit(solution)/shard_map/all_gather | solution.py:50
  9.8 18.5 %copy-start.2 = (bf16[1,5,128,1024]{3,2,1,0:T(8,128)(2,1)S(1)}, bf16[1,5,128,1024]{3,2,1,0:T(8,128)(2,1)}, u32[]{:S(2)}) copy-start(bf16[1,5,128,1024]{3,2,1,0:T(8,128)(2,1)} %param.7) | copy-start | bytes 3932164
  28.2 75.2 %all-gather.15.cloned.1.call-start = ((), (), s32[]{:S(2)}) async-start(), calls=%async_computation.4 | async-start | bytes 7077888 | tf_op jit(solution)/shard_map/all_gather | solution.py:24
  28.4 20.8 %copy-start.3 = (bf16[1,5,128,1024]{3,2,1,0:T(8,128)(2,1)S(1)}, bf16[1,5,128,1024]{3,2,1,0:T(8,128)(2,1)}, u32[]{:S(2)}) copy-start(bf16[1,5,128,1024]{3,2,1,0:T(8,128)(2,1)} %param.6) | copy-start | bytes 3932164
  28.5 19.7 %collective-permute-start.1 = (bf16[3,128,1024]{2,1,0:T(8,128)(2,1)S(1)}, bf16[3,128,1024]{2,1,0:T(8,128)(2,1)S(1)}, u32[]{:S(2)}, u32[]{:S(2)}) collective-permute-start(bf16[3,128,1024]{2,1,0:T(8,128)(2,1)S(1)} %pad_maximum_fusion.1), channel_id=1, source_target_pairs={{0,24},{8,0},{16,8},{24,16},{1,25},{9,1},{17,9},{25,17},{2,26},{10... | collective-permute-start | bytes 2359304 | tf_op jit(solution)/shard_map/ppermute | solution.py:14
  48.2 0.9 copy-start.4
  49.1 122.3 %all-gather.9.cloned.1.call-start = ((), (), s32[]{:S(2)}) async-start(), calls=%async_computation.1 | async-start | bytes 2359296 | tf_op jit(solution)/shard_map/all_gather | solution.py:50
  49.3 18.1 %collective-permute-start = (bf16[3,128,1024]{2,1,0:T(8,128)(2,1)S(1)}, bf16[3,128,1024]{2,1,0:T(8,128)(2,1)S(1)}, u32[]{:S(2)}, u32[]{:S(2)}) collective-permute-start(bf16[3,128,1024]{2,1,0:T(8,128)(2,1)S(1)} %pad_maximum_fusion), channel_id=1, source_target_pairs={{0,8},{8,16},{16,24},{24,0},{1,9},{9,17},{17,25},{25,1},{2,10},{10... | collective-permute-start | bytes 2359304 | tf_op jit(solution)/shard_map/ppermute | solution.py:14
  109.8 4.0 %copy-start = (bf16[5120,1024]{1,0:T(8,128)(2,1)}, bf16[5120,1024]{1,0:T(8,128)(2,1)S(1)}, u32[]{:S(2)}) copy-start(bf16[5120,1024]{1,0:T(8,128)(2,1)S(1)} %constant_dynamic-update-slice_fusion) | copy-start | bytes 31457284
  143.4 95.3 %all-gather.11.cloned.1.call-start = ((), (), s32[]{:S(2)}) async-start(), calls=%async_computation.2 | async-start | bytes 2359296 | tf_op jit(solution)/shard_map/all_gather | solution.py:50
  210.8 95.3 %all-gather.13.cloned.1.call-start = ((), (), s32[]{:S(2)}) async-start(), calls=%async_computation.3 | async-start | bytes 2359296 | tf_op jit(solution)/shard_map/all_gather | solution.py:50
Sparse Core Ops, SparseCore 0:
  28.3 27.1 all-gather.6
  58.0 45.3 all-gather.14
  143.6 27.7 all-gather.8
  210.9 27.7 all-gather.10
  278.3 27.7 all-gather.12
